TPU v7x, 32 devices: a whole 2x2x4 slice. The times are simulated.
32 devices in a mesh: orb: 4 (over z), tile: 8 (over y, x, core).
Axes of the slice: x: 2, y: 2, z: 4, core: 2. Of those that a mesh axis runs over, the one named last changes fastest.
Arguments:
- basis_values: bfloat16 [2048, 65536], P('tile'), may hold values from -6 to 6
- coefficients: bfloat16 [65536, 128], P('tile', 'orb'), may hold values from -0.03125 to 0.03125
- occupations: float32 [128], P('orb'), may hold values from 0.5 to 2
- owners: int32 [2048, 1], P('tile'), may hold values from 0 to 7; in each aligned block of 256 rows (0 to 255, 256 to 511, ...) at most 64 rows name the same one
- offsets: int32 [2048], P('tile'), may hold values from 0 to 8191
Outputs:
- density: float32 [64, 64, 128], P('tile', 'orb')
- gradient: float32 [3, 64, 64, 128], P(None, 'tile', 'orb')
Inputs may be any that keep to these rules, and one draw needn't show every extreme that they name: `owners`: at most 64 entries of one tile's list name the same owner, and some tile's list reaches 64.
All inputs are finite; a program needn't handle non-finite values.
Results may differ from a plain program's by a relative error of at most 0.0003.
Values may be sent and summed in bfloat16 or wider, within the bound.
A program may use at most 320 MiB of HBM per device.

v0:
```python
import jax
import jax.numpy as jnp
from jax import lax
from jax.sharding import PartitionSpec as P

CY = 64
CZ = 128


def with_halo(cells, sides, width):
    for axis, dim in sides:
        count = lax.axis_size(axis)
        ends = count - 1
        head = lax.slice_in_dim(cells, 0, width, axis=dim)
        tail = lax.slice_in_dim(cells, cells.shape[dim] - width, cells.shape[dim], axis=dim)
        cells = jnp.concatenate(
            [
                lax.ppermute(tail, axis, [(i, (i + 1) % count) for i in range(ends)]),
                cells,
                lax.ppermute(head, axis, [((i + 1) % count, i) for i in range(ends)]),
            ],
            axis=dim,
        )
    return cells


def central(padded):
    along_x = 0.5 * (padded[2:, 1:-1, 1:-1] - padded[:-2, 1:-1, 1:-1])
    along_y = 0.5 * (padded[1:-1, 2:, 1:-1] - padded[1:-1, :-2, 1:-1])
    along_z = 0.5 * (padded[1:-1, 1:-1, 2:] - padded[1:-1, 1:-1, :-2])
    return jnp.stack([along_x, along_y, along_z])


def body(basis_values, coefficients, occupations, owners, offsets):
    listed_count = owners.shape[0]
    rows_held = coefficients.shape[0]
    local_orbitals = coefficients.shape[1]
    owner_ids = owners[:, 0]
    global_rows = owner_ids * rows_held + offsets
    empty = jnp.zeros((listed_count, local_orbitals), jnp.bfloat16)
    shard_rows = lax.all_gather(coefficients, "tile", axis=0, tiled=True)
    inside = (global_rows >= 0) & (global_rows < shard_rows.shape[0])
    safe_rows = jnp.clip(global_rows, 0, shard_rows.shape[0] - 1)
    taken = jnp.take(shard_rows, safe_rows, axis=0)
    listed = jnp.where(inside[:, None], taken, empty)
    depth_cells = basis_values.shape[1] // (CY * CZ)
    share_width = CY // lax.axis_size("orb")
    orbitals = jnp.einsum("bo,bc->oc", listed, basis_values, preferred_element_type=jnp.float32)
    partial_value = jnp.sum(occupations[:, None] * orbitals * orbitals, axis=0).reshape(
        depth_cells, CY, CZ
    )
    density_full = lax.psum(partial_value, "orb")
    padded = with_halo(density_full, (("tile", 0),), 1)
    padded = jnp.pad(padded, ((0, 0), (1, 1), (1, 1)))
    first_col = lax.axis_index("orb") * share_width
    density = lax.dynamic_slice_in_dim(density_full, first_col, share_width, 1)
    gradient = lax.dynamic_slice_in_dim(central(padded), first_col, share_width, 2)
    return (density, gradient)


def solution(mesh):
    placed = (P("tile", None), P("tile", "orb"), P("orb"), P("tile", None), P("tile"))
    return jax.shard_map(
        body,
        mesh=mesh,
        in_specs=placed,
        out_specs=(P("tile", "orb", None), P(None, "tile", "orb", None)),
        check_vma=False,
    )
```

profile of v0, /device:TPU:0, one launch (start us, length us, event | category | flops | bytes accessed | tf_op | source)
XLA Modules:
  0.0 181.1 jit_solution(3366293693858491619)
XLA Ops:
  7.2 0.0 all-gather.2.cloned.1.call-start
  7.2 2.7 %copy.7 = bf16[8192,32]{1,0:T(8,128)(2,1)} copy(bf16[8192,32]{0,1:T(8,128)(2,1)} %param.6) | data formatting | bytes 1048576 | tf_op args[1]
  9.9 0.0 all-gather.2.cloned.1.call-update
  9.9 0.0 all-reduce.3.cloned.1.call-start
  10.0 0.7 broadcast_multiply_fusion
  10.6 0.7 compare_and_fusion
  11.3 91.2 %all-gather.2.cloned.1.call-done = bf16[65536,32]{1,0:T(8,128)(2,1)} async-done(((bf16[8192,32]{1,0:T(8,128)(2,1)}), bf16[65536,32]{1,0:T(8,128)(2,1)}) %all-gather.2.cloned.1.call-update) | async-done | bytes 4194320 | tf_op jit(solution)/shard_map/all_gather | solution.py:41
  102.5 8.7 %gather_fusion = bf16[256,32]{1,0:T(8,128)(2,1)S(1)} fusion(bf16[65536,32]{1,0:T(8,128)(2,1)} %all-gather.2.cloned.1.call-done, s32[1024]{0:T(1024)S(1)} %pad_clamp_fusion), kind=kCustom, calls=%fused_computation | custom fusion | bytes 33792 | tf_op jit(solution)/shard_map/jit(_take)/gather | solution.py:44
  111.2 17.4 %fusion = f32[65536]{0:T(1024)} fusion(f32[32]{0:T(128)} %param.7, bf16[256,65536]{1,0:T(8,128)(2,1)} %param.5, bf16[256,32]{1,0:T(8,128)(2,1)S(1)} %gather_fusion, pred[256]{0:T(512)(128)(4,1)S(1)} %get-tuple-element.2, pred[256]{0:T(512)(128)(4,1)S(1)} %get-tuple-element.8), kind=kOutput, calls=%fused_computation.2 | convolution fusion | flops 1079984128 | bytes 33833600 | tf_op jit(solution)/shard_map/bo,bc->oc/dot_general | solution.py:48
  128.6 0.0 all-reduce.3.cloned.1.call-update
  128.6 35.7 %all-reduce.3.cloned.1.call-done = f32[8,64,128]{2,1,0:T(8,128)} async-done(((f32[8,64,128]{2,1,0:T(8,128)}), f32[8,64,128]{2,1,0:T(8,128)}) %all-reduce.3.cloned.1.call-update) | async-done | bytes 262160 | tf_op jit(solution)/shard_map/psum | solution.py:52
  164.4 0.8 fusion.24
  165.1 1.3 collective-permute-start
  166.4 3.0 %collective-permute-start.1 = (f32[1,64,128]{2,1,0:T(8,128)S(1)}, f32[1,64,128]{2,1,0:T(8,128)S(1)}, u32[]{:S(2)}, u32[]{:S(2)}) collective-permute-start(f32[1,64,128]{2,1,0:T(8,128)S(1)} %get-tuple-element.7), channel_id=1, source_target_pairs={{0,1},{1,2},{2,3},{3,4},{4,5},{5,6},{6,7},{8,9},{9,10},{10,11},{11... | collective-permute-start | bytes 98312 | tf_op jit(solution)/shard_map/ppermute | solution.py:18
  169.5 1.5 constant_dynamic-slice_fusion
  171.0 0.0 collective-permute-done
  171.0 0.0 collective-permute-done.1
  171.0 1.2 select_maximum_fusion
  172.2 1.3 fusion.5
  173.5 0.7 fusion.12
  (1 shorter events, 0.0 us)
Async XLA Ops:
  7.2 95.4 %all-gather.2.cloned.1.call-start = ((), (), s32[]{:S(2)}) async-start(), calls=%async_computation | async-start | bytes 18874368 | tf_op jit(solution)/shard_map/all_gather | solution.py:41
  9.9 154.4 %all-reduce.3.cloned.1.call-start = ((), (), s32[]{:S(2)}) async-start(), calls=%async_computation.1 | async-start | bytes 524288 | tf_op jit(solution)/shard_map/psum | solution.py:52
  165.1 5.8 %collective-permute-start = (f32[1,64,128]{2,1,0:T(8,128)S(1)}, f32[1,64,128]{2,1,0:T(8,128)S(1)}, u32[]{:S(2)}, u32[]{:S(2)}) collective-permute-start(f32[1,64,128]{2,1,0:T(8,128)S(1)} %get-tuple-element.6), channel_id=1, source_target_pairs={{1,0},{2,1},{3,2},{4,3},{5,4},{6,5},{7,6},{9,8},{10,9},{11,10},{12... | collective-permute-start | bytes 98312 | tf_op jit(solution)/shard_map/ppermute | solution.py:20
  166.4 4.5 %collective-permute-start.1 = (f32[1,64,128]{2,1,0:T(8,128)S(1)}, f32[1,64,128]{2,1,0:T(8,128)S(1)}, u32[]{:S(2)}, u32[]{:S(2)}) collective-permute-start(f32[1,64,128]{2,1,0:T(8,128)S(1)} %get-tuple-element.7), channel_id=1, source_target_pairs={{0,1},{1,2},{2,3},{3,4},{4,5},{5,6},{6,7},{8,9},{9,10},{10,11},{11... | collective-permute-start | bytes 98312 | tf_op jit(solution)/shard_map/ppermute | solution.py:18
Sparse Core Ops, SparseCore 0:
  10.0 92.4 all-gather.1
  128.7 35.5 all-reduce.2
where the time goes:
time: 182 us; the launch traced here: 181 us
  waiting for transfers between devices  127 us (70%)
  matrix products  17.4 us (10%)
  between operations  14.1 us (8%)
  local copies, waits for them, and re-layouts  13.6 us (7%)
  other arithmetic  4.62 us (3%)
  starting transfers between devices  4.39 us (2%)
    all_gather x1, waiting for transfers between devices, body(): shard_rows = lax.all_gather(coefficients, 'tile', axis=0, tiled=True)  91.2 us
    psum x1, waiting for transfers between devices, body(): density_full = lax.psum(partial_value, 'orb')  35.7 us
    dot_general x1, matrix products, body(): jnp.einsum('bo,bc->oc', listed, basis_values, preferred_element_type=jnp....  17.4 us
    gather x1, local copies, waits for them, and re-layouts, body(): taken = jnp.take(shard_rows, safe_rows, axis=0)  8.65 us
  transfers between devices with their start and end apart: 4, of which 2 were waited for; matrix products, arithmetic and copies ran while one was open for 2% of the time, Pallas kernels for 0%

commit v1 on v0

v1 whole, which is shorter than its diff:
```python
import functools

import jax
import jax.numpy as jnp
from jax import lax
from jax.experimental import pallas as pl
from jax.experimental.pallas import tpu as pltpu
from jax.sharding import PartitionSpec as P

CY = 64
CZ = 128
LANES = 128
MESH = pl.DeviceIdType.MESH
F32 = jnp.float32
BF16 = jnp.bfloat16


def iota(shape, dim):
    return lax.broadcasted_iota(jnp.int32, shape, dim)


def kernel(
    n, m, owners_ref, offsets_ref, occ_ref, coef_ref, basis_ref, dens_ref, grad_ref,
    slabs, coef, req_out, req_in, picked, rows, place, occ_in, listed, dens,
    slab_sem, coef_sem, req_send, req_recv, row_send, row_recv,
    occ_send, occ_recv, list_send, list_recv, halo_send, halo_recv,
):
    t = lax.axis_index("tile")
    o = lax.axis_index("orb")
    nbt = owners_ref.shape[1]
    held = coef_ref.shape[1]
    loc = coef_ref.shape[0]
    depth = basis_ref.shape[1] // (CY * CZ)
    width = CY // m
    inner = width * CZ
    cap = 2 * nbt // n
    per = LANES // cap
    groups = n // per
    order = [0, depth - 1] + list(range(1, depth - 1))

    coef_copy = pltpu.make_async_copy(coef_ref, coef, coef_sem)
    coef_copy.start()
    low = (o * width + CY - 1) % CY
    high = (o * width + width) % CY

    def slab_copies(x):
        out = []
        for k, (row, count, at) in enumerate(
            ((o * width, width, CZ), (low, 1, 0), (high, 1, CZ + inner))
        ):
            src = basis_ref.at[:, pl.ds(pl.multiple_of((x * CY + row) * CZ, CZ), count * CZ)]
            dst = slabs.at[x, :, pl.ds(at, count * CZ)]
            out.append(pltpu.make_async_copy(src, dst, slab_sem.at[x, k]))
        return out

    for x in order:
        for copy in slab_copies(x):
            copy.start()

    dens[0] = jnp.zeros(dens.shape[1:], F32)
    dens[depth + 1] = jnp.zeros(dens.shape[1:], F32)

    barrier = pltpu.get_barrier_semaphore()
    for d in range(1, n):
        pl.semaphore_signal(barrier, inc=1, device_id={"tile": (t + d) % n}, device_id_type=MESH)
    for d in range(1, m):
        pl.semaphore_signal(barrier, inc=1, device_id={"orb": (o + d) % m}, device_id_type=MESH)

    own = owners_ref[...]
    off = offsets_ref[...]
    named = own == iota((n, nbt), 0)
    before = (iota((nbt, nbt), 0) < iota((nbt, nbt), 1)).astype(F32).astype(BF16)
    rank = jnp.dot(named.astype(F32).astype(BF16), before, preferred_element_type=F32)
    slot = jnp.sum(jnp.where(named, rank, 0.0), axis=0, keepdims=True).astype(jnp.int32)
    slot = slot + (t % per) * cap
    spot = (slot == iota((LANES, nbt), 0)).astype(F32).astype(BF16)
    named_f = named.astype(F32)
    high_part = (named_f * (off // LANES).astype(F32)).astype(BF16)
    low_part = (named_f * (off % LANES).astype(F32)).astype(BF16)
    nt = (((1,), (1,)), ((), ()))
    req_high = lax.dot_general(high_part, spot, nt, preferred_element_type=F32)
    req_low = lax.dot_general(low_part, spot, nt, preferred_element_type=F32)
    req = (req_high * float(LANES) + req_low).astype(jnp.int32)
    for d in range(n):
        req_out[d] = jnp.broadcast_to(req[d:d + 1], (8, LANES))
    req_in[t] = req_out[t]
    row_pad = jnp.concatenate([occ_ref[...], jnp.zeros((1, LANES - loc), F32)], axis=1)
    occ_in[o] = jnp.broadcast_to(row_pad, (8, LANES))

    pl.semaphore_wait(barrier, n + m - 2)

    def req_copy(src, dst):
        return pltpu.make_async_remote_copy(
            src_ref=req_out.at[dst], dst_ref=req_in.at[src], send_sem=req_send.at[dst],
            recv_sem=req_recv.at[src], device_id={"tile": dst}, device_id_type=MESH)

    def occ_copy(src, dst):
        return pltpu.make_async_remote_copy(
            src_ref=occ_in.at[src], dst_ref=occ_in.at[src], send_sem=occ_send.at[dst],
            recv_sem=occ_recv.at[src], device_id={"orb": dst}, device_id_type=MESH)

    def row_copy(src, dst):
        return pltpu.make_async_remote_copy(
            src_ref=picked.at[dst // per],
            dst_ref=rows.at[:, pl.ds(pl.multiple_of(src * LANES, LANES), LANES)],
            send_sem=row_send.at[dst], recv_sem=row_recv.at[src],
            device_id={"tile": dst}, device_id_type=MESH)

    def list_copy(src, dst):
        return pltpu.make_async_remote_copy(
            src_ref=listed.at[src], dst_ref=listed.at[src], send_sem=list_send.at[dst],
            recv_sem=list_recv.at[src], device_id={"orb": dst}, device_id_type=MESH)

    for d in range(1, n):
        req_copy(t, (t + d) % n).start()
    for d in range(1, m):
        occ_copy(o, (o + d) % m).start()

    key = own * LANES + slot
    for d in range(n):
        here = key == iota((LANES, nbt), 0) + d * LANES
        place[d * LANES:(d + 1) * LANES, :] = here.astype(F32).astype(BF16)

    coef_copy.wait()
    for d in range(1, n):
        req_copy((t + d) % n, t).wait_recv()

    wanted = []
    for g in range(groups):
        total = req_in[g * per]
        for k in range(1, per):
            total = total + req_in[g * per + k]
        wanted.append(total)
    lane = [w % LANES for w in wanted]
    chunk_of = [w // LANES for w in wanted]
    parts = loc // 8

    def pick(h, accs):
        block = coef[:, pl.ds(pl.multiple_of(h * LANES, LANES), LANES)].astype(F32)
        out = []
        for g in range(groups):
            hit = chunk_of[g] == h
            for p in range(parts):
                got = jnp.take_along_axis(
                    block[p * 8:(p + 1) * 8], lane[g], axis=1, mode="promise_in_bounds")
                out.append(jnp.where(hit, got, accs[g * parts + p]))
        return tuple(out)

    accs = lax.fori_loop(
        0, held // LANES, pick, (jnp.zeros((8, LANES), F32),) * (groups * parts), unroll=4)
    for g in range(groups):
        picked[g] = jnp.concatenate(accs[g * parts:(g + 1) * parts], axis=0).astype(BF16)
    for d in range(1, n):
        row_copy(t, (t + d) % n).start()
    rows[:, pl.ds(pl.multiple_of(t * LANES, LANES), LANES)] = picked[t // per]
    for d in range(1, n):
        row_copy((t + d) % n, t).wait_recv()

    placed = jnp.dot(rows[...], place[...], preferred_element_type=F32)
    listed[o] = placed.astype(BF16)
    for d in range(1, m):
        list_copy(o, (o + d) % m).start()

    for d in range(1, m):
        occ_copy((o + d) % m, o).wait_recv()
    diagonal = iota((loc, LANES), 0) == iota((loc, LANES), 1)
    occ = jnp.concatenate(
        [jnp.sum(jnp.where(diagonal, occ_in[k, 0:1, :], 0.0), axis=1, keepdims=True)
         for k in range(m)], axis=0)
    occ = jnp.broadcast_to(occ, (m * loc, LANES))

    for d in range(1, m):
        list_copy((o + d) % m, o).wait_recv()
    left = listed[...].reshape(m * loc, nbt)
    count = width + 2

    def slab(x):
        for copy in slab_copies(x):
            copy.wait()
        for c in range(0, count, 2):
            orbitals = jnp.dot(
                left, slabs[x, :, c * CZ:(c + 2) * CZ], preferred_element_type=F32)
            for k in range(2):
                half = orbitals[:, k * CZ:(k + 1) * CZ]
                line = jnp.sum(half * half * occ, axis=0, keepdims=True)
                if c + k == 0:
                    line = jnp.where(o == 0, 0.0, line)
                if c + k == count - 1:
                    line = jnp.where(o == m - 1, 0.0, line)
                dens[x + 1, 7 + c + k:8 + c + k, :] = line

    def halo_copy(up):
        dst = t + 1 if up else t - 1
        return pltpu.make_async_remote_copy(
            src_ref=dens.at[depth if up else 1, pl.ds(8, width)],
            dst_ref=dens.at[0 if up else depth + 1, pl.ds(8, width)],
            send_sem=halo_send.at[int(up)], recv_sem=halo_recv.at[int(up)],
            device_id={"tile": (dst + n) % n}, device_id_type=MESH)

    slab(0)

    @pl.when(t > 0)
    def _():
        halo_copy(False).start()

    slab(depth - 1)

    @pl.when(t < n - 1)
    def _():
        halo_copy(True).start()

    def middle(x, _):
        slab(x)
        return 0

    lax.fori_loop(1, depth - 1, middle, 0)

    def gradient(x):
        rest = dens[x + 1, 8:8 + width, :]
        dens_ref[x] = rest
        grad_ref[0, x] = 0.5 * (dens[x + 2, 8:8 + width, :] - dens[x, 8:8 + width, :])
        grad_ref[1, x] = 0.5 * (dens[x + 1, 9:9 + width, :] - dens[x + 1, 7:7 + width, :])
        z = iota((width, CZ), 1)
        after = jnp.where(z == CZ - 1, 0.0, pltpu.roll(rest, CZ - 1, 1))
        prior = jnp.where(z == 0, 0.0, pltpu.roll(rest, 1, 1))
        grad_ref[2, x] = 0.5 * (after - prior)

    for x in range(1, depth - 1):
        gradient(x)

    @pl.when(t < n - 1)
    def _():
        halo_copy(False).wait_recv()

    @pl.when(t > 0)
    def _():
        halo_copy(True).wait_recv()

    gradient(0)
    gradient(depth - 1)

    for d in range(1, n):
        req_copy(t, (t + d) % n).wait_send()
        row_copy(t, (t + d) % n).wait_send()
    for d in range(1, m):
        occ_copy(o, (o + d) % m).wait_send()
        list_copy(o, (o + d) % m).wait_send()

    @pl.when(t > 0)
    def _():
        halo_copy(False).wait_send()

    @pl.when(t < n - 1)
    def _():
        halo_copy(True).wait_send()


def body(n, m, basis_values, coefficients, occupations, owners, offsets):
    nbt = owners.shape[0]
    held, loc = coefficients.shape
    depth = basis_values.shape[1] // (CY * CZ)
    width = CY // m
    groups = n // (LANES * n // (2 * nbt))
    dma = pltpu.SemaphoreType.DMA
    vmem = pl.BlockSpec(memory_space=pltpu.VMEM)
    hbm = pl.BlockSpec(memory_space=pl.ANY)
    return pl.pallas_call(
        functools.partial(kernel, n, m),
        out_shape=(
            jax.ShapeDtypeStruct((depth, width, CZ), F32),
            jax.ShapeDtypeStruct((3, depth, width, CZ), F32),
        ),
        in_specs=[vmem, vmem, vmem, hbm, hbm],
        out_specs=(vmem, vmem),
        scratch_shapes=[
            pltpu.VMEM((depth, nbt, (width + 2) * CZ), BF16),
            pltpu.VMEM((loc, held), BF16),
            pltpu.VMEM((n, 8, LANES), jnp.int32),
            pltpu.VMEM((n, 8, LANES), jnp.int32),
            pltpu.VMEM((groups, loc, LANES), BF16),
            pltpu.VMEM((loc, n * LANES), BF16),
            pltpu.VMEM((n * LANES, nbt), BF16),
            pltpu.VMEM((m, 8, LANES), F32),
            pltpu.VMEM((m, loc, nbt), BF16),
            pltpu.VMEM((depth + 2, width + 16, CZ), F32),
            dma((depth, 3)), dma(()),
            dma((n,)), dma((n,)), dma((n,)), dma((n,)),
            dma((m,)), dma((m,)), dma((m,)), dma((m,)),
            dma((2,)), dma((2,)),
        ],
        compiler_params=pltpu.CompilerParams(collective_id=0, has_side_effects=True),
    )(
        owners.reshape(1, nbt), offsets.reshape(1, nbt), occupations.reshape(1, loc),
        coefficients.T, basis_values,
    )


def solution(mesh):
    n, m = mesh.shape["tile"], mesh.shape["orb"]
    placed = (P("tile", None), P("tile", "orb"), P("orb"), P("tile", None), P("tile"))
    return jax.shard_map(
        functools.partial(body, n, m),
        mesh=mesh,
        in_specs=placed,
        out_specs=(P("tile", "orb", None), P(None, "tile", "orb", None)),
        check_vma=False,
    )
```

time: 182 us -> 27.2 us (0.15)
  waiting for transfers between devices: 127 us -> 0 us
  Pallas kernels: 0 us -> 23.2 us
  matrix products: 17.4 us -> 0 us
  between operations: 14.1 us -> 0.64 us
  local copies, waits for them, and re-layouts: 13.6 us -> 3.09 us
  other arithmetic: 4.62 us -> 0 us
  starting transfers between devices: 4.39 us -> 0 us
    all_gather x1 -> x0, waiting for transfers between devices: 91.2 us -> none  [body(): shard_rows = lax.all_gather(coefficients, 'tile', axis=0, tiled=True)]
    psum x1 -> x0, waiting for transfers between devices: 35.7 us -> none  [body(): density_full = lax.psum(partial_value, 'orb')]
    pallas_call x0 -> x1, Pallas kernels: none -> 23.2 us  [body(): pl.pallas_call(functools.partial(kernel, n, m), out_shape=(jax.ShapeDtype...]
    dot_general x1 -> x0, matrix products: 17.4 us -> none  [body(): jnp.einsum('bo,bc->oc', listed, basis_values, preferred_element_type=jnp....]
    gather x1 -> x0, local copies, waits for them, and re-layouts: 8.65 us -> none  [body(): taken = jnp.take(shard_rows, safe_rows, axis=0)]
    ppermute x2 -> x0, starting transfers between devices: 4.31 us -> none  [the longest x1 3.03 us: with_halo(): lax.ppermute(tail, axis, [(i, (i + 1) % count) for i in range(ends)])]
    another operation x2 -> x0, other arithmetic: 2.03 us -> none  [central(): return jnp.stack([along_x, along_y, along_z])]
  transfers between devices with their start and end apart: 4 -> 0, of which waited for: 2 -> 0; matrix products, arithmetic and copies ran while one was open for 2% -> 0% of each run, Pallas kernels for 0% -> 0%
where the time goes in v1:
time: 27.2 us; the launch traced here: 26.9 us
  Pallas kernels  23.2 us (85%)
  local copies, waits for them, and re-layouts  3.09 us (11%)
  between operations  0.64 us (2%)
    pallas_call x1, Pallas kernels, body(): pl.pallas_call(functools.partial(kernel, n, m), out_shape=(jax.ShapeDtype...  23.2 us
    unnamed x2, local copies, waits for them, and re-layouts  3.09 us

profile of v1, /device:TPU:0, one launch (start us, length us, event | category | flops | bytes accessed | tf_op | source)
XLA Modules:
  0.0 26.9 jit_solution(10724200367331567350)
XLA Ops:
  0.6 23.2 %shard_map.68 = (f32[8,16,128]{2,1,0:T(8,128)}, f32[3,8,16,128]{3,2,1,0:T(8,128)}) custom-call(s32[1,256]{1,0:T(1,128)} %bitcast.5, s32[1,256]{1,0:T(1,128)} %bitcast.6, f32[1,32]{1,0:T(1,128)} %bitcast.7, bf16[32,8192]{1,0:T(8,128)(2,1)} %bitcast.4, bf16[256,65536]{1,0:T(8,128)(2,1)} %basis_ref.1), custom_call_target="tpu_custom_call" | custom-call | tf_op jit(solution)/shard_map/pallas_call | solution.py:267
  23.9 1.5 %copy.9 = f32[8,16,128]{2,1,0:T(8,128)} copy(f32[8,16,128]{2,1,0:T(8,128)} %get-tuple-element.4) | data formatting | bytes 131072
  25.3 1.6 %copy.10 = f32[3,8,16,128]{3,2,1,0:T(8,128)} copy(f32[3,8,16,128]{3,2,1,0:T(8,128)} %get-tuple-element.5) | data formatting | bytes 393216

commit v2 on v1

--- a/solution.py
+++ b/solution.py
@@ -21,9 +21,9 @@
 
 def kernel(
     n, m, owners_ref, offsets_ref, occ_ref, coef_ref, basis_ref, dens_ref, grad_ref,
-    slabs, coef, req_out, req_in, picked, rows, place, occ_in, listed, dens,
-    slab_sem, coef_sem, req_send, req_recv, row_send, row_recv,
-    occ_send, occ_recv, list_send, list_recv, halo_send, halo_recv,
+    own_in, off_in, occ_own, slabs, coef, req_out, req_in, picked, rows, place, occ_in, listed, dens,
+    small_sem, slab_sem, coef_sem, req_send, req_recv, row_send, row_recv,
+    occ_send, occ_recv, list_send, list_recv, halo_send, halo_recv, ready,
 ):
     t = lax.axis_index("tile")
     o = lax.axis_index("orb")
@@ -38,6 +38,31 @@
     groups = n // per
     order = [0, depth - 1] + list(range(1, depth - 1))
 
+    dens[0] = jnp.zeros(dens.shape[1:], F32)
+    dens[depth + 1] = jnp.zeros(dens.shape[1:], F32)
+
+    beside = ((o > 0, -1), (o < m - 1, 1))
+    count_beside = jnp.where(o > 0, 1, 0) + jnp.where(o < m - 1, 1, 0)
+
+    def tell_beside(sem):
+        for has, step in beside:
+            @pl.when(has)
+            def _():
+                pl.semaphore_signal(
+                    sem, inc=1, device_id={"orb": (o + step + m) % m}, device_id_type=MESH)
+
+    barrier = pltpu.get_barrier_semaphore()
+    for d in range(1, n):
+        pl.semaphore_signal(barrier, inc=1, device_id={"tile": (t + d) % n}, device_id_type=MESH)
+    tell_beside(barrier)
+
+    small = [
+        pltpu.make_async_copy(src, dst, small_sem.at[k])
+        for k, (src, dst) in enumerate(
+            ((owners_ref, own_in), (offsets_ref, off_in), (occ_ref, occ_own)))
+    ]
+    for copy in small:
+        copy.start()
     coef_copy = pltpu.make_async_copy(coef_ref, coef, coef_sem)
     coef_copy.start()
     low = (o * width + CY - 1) % CY
@@ -57,17 +82,10 @@
         for copy in slab_copies(x):
             copy.start()
 
-    dens[0] = jnp.zeros(dens.shape[1:], F32)
-    dens[depth + 1] = jnp.zeros(dens.shape[1:], F32)
-
-    barrier = pltpu.get_barrier_semaphore()
-    for d in range(1, n):
-        pl.semaphore_signal(barrier, inc=1, device_id={"tile": (t + d) % n}, device_id_type=MESH)
-    for d in range(1, m):
-        pl.semaphore_signal(barrier, inc=1, device_id={"orb": (o + d) % m}, device_id_type=MESH)
-
-    own = owners_ref[...]
-    off = offsets_ref[...]
+    for copy in small:
+        copy.wait()
+    own = own_in[...]
+    off = off_in[...]
     named = own == iota((n, nbt), 0)
     before = (iota((nbt, nbt), 0) < iota((nbt, nbt), 1)).astype(F32).astype(BF16)
     rank = jnp.dot(named.astype(F32).astype(BF16), before, preferred_element_type=F32)
@@ -84,10 +102,10 @@
     for d in range(n):
         req_out[d] = jnp.broadcast_to(req[d:d + 1], (8, LANES))
     req_in[t] = req_out[t]
-    row_pad = jnp.concatenate([occ_ref[...], jnp.zeros((1, LANES - loc), F32)], axis=1)
+    row_pad = jnp.concatenate([occ_own[...], jnp.zeros((1, LANES - loc), F32)], axis=1)
     occ_in[o] = jnp.broadcast_to(row_pad, (8, LANES))
 
-    pl.semaphore_wait(barrier, n + m - 2)
+    pl.semaphore_wait(barrier, n - 1 + count_beside)
 
     def req_copy(src, dst):
         return pltpu.make_async_remote_copy(
@@ -99,9 +117,9 @@
             src_ref=occ_in.at[src], dst_ref=occ_in.at[src], send_sem=occ_send.at[dst],
             recv_sem=occ_recv.at[src], device_id={"orb": dst}, device_id_type=MESH)
 
-    def row_copy(src, dst):
-        return pltpu.make_async_remote_copy(
-            src_ref=picked.at[dst // per],
+    def row_copy(turn, src, dst):
+        return pltpu.make_async_remote_copy(
+            src_ref=picked.at[turn],
             dst_ref=rows.at[:, pl.ds(pl.multiple_of(src * LANES, LANES), LANES)],
             send_sem=row_send.at[dst], recv_sem=row_recv.at[src],
             device_id={"tile": dst}, device_id_type=MESH)
@@ -113,8 +131,8 @@
 
     for d in range(1, n):
         req_copy(t, (t + d) % n).start()
-    for d in range(1, m):
-        occ_copy(o, (o + d) % m).start()
+    if m > 2:
+        tell_beside(ready.at[0])
 
     key = own * LANES + slot
     for d in range(n):
@@ -122,39 +140,54 @@
         place[d * LANES:(d + 1) * LANES, :] = here.astype(F32).astype(BF16)
 
     coef_copy.wait()
+
+    home = t // per
+    turns = [home, home + 1 - 2 * (home % 2), (home + 2) % groups, groups - 1 - home]
+    wide = 2 * LANES
+    batch = 8
+    for turn, g in enumerate(turns):
+        members = [g * per + k for k in range(per)]
+        total = None
+        for who in members:
+            if turn == 0:
+                @pl.when(who != t)
+                def _():
+                    req_copy(who, t).wait_recv()
+            else:
+                req_copy(who, t).wait_recv()
+            total = req_in[who] if total is None else total + req_in[who]
+        chunk_of = total // wide
+        lane = (total % wide)[0:1]
+        chosen = (iota((wide, LANES), 0) == lane).astype(F32).astype(BF16)
+        acc = [jnp.zeros((8, LANES), F32)] * (loc // 8)
+        for first in range(0, held // wide, batch):
+            stack = jnp.concatenate(
+                [coef[:, h * wide:(h + 1) * wide] for h in range(first, first + batch)], axis=0)
+            found = jnp.dot(stack, chosen, preferred_element_type=F32)
+            for h in range(batch):
+                hit = chunk_of == first + h
+                for p in range(loc // 8):
+                    at = h * loc + p * 8
+                    acc[p] = jnp.where(hit, found[at:at + 8], acc[p])
+        picked[turn] = jnp.concatenate(acc, axis=0).astype(BF16)
+        for who in members:
+            if turn == 0:
+                @pl.when(who != t)
+                def _():
+                    row_copy(turn, t, who).start()
+            else:
+                row_copy(turn, t, who).start()
+    rows[:, pl.ds(pl.multiple_of(t * LANES, LANES), LANES)] = picked[0]
+
+    for k in range(m - 2):
+        pl.semaphore_wait(ready.at[k], count_beside)
+        if k + 1 < m - 2:
+            tell_beside(ready.at[k + 1])
+    for d in range(1, m):
+        occ_copy(o, (o + d) % m).start()
+
     for d in range(1, n):
-        req_copy((t + d) % n, t).wait_recv()
-
-    wanted = []
-    for g in range(groups):
-        total = req_in[g * per]
-        for k in range(1, per):
-            total = total + req_in[g * per + k]
-        wanted.append(total)
-    lane = [w % LANES for w in wanted]
-    chunk_of = [w // LANES for w in wanted]
-    parts = loc // 8
-
-    def pick(h, accs):
-        block = coef[:, pl.ds(pl.multiple_of(h * LANES, LANES), LANES)].astype(F32)
-        out = []
-        for g in range(groups):
-            hit = chunk_of[g] == h
-            for p in range(parts):
-                got = jnp.take_along_axis(
-                    block[p * 8:(p + 1) * 8], lane[g], axis=1, mode="promise_in_bounds")
-                out.append(jnp.where(hit, got, accs[g * parts + p]))
-        return tuple(out)
-
-    accs = lax.fori_loop(
-        0, held // LANES, pick, (jnp.zeros((8, LANES), F32),) * (groups * parts), unroll=4)
-    for g in range(groups):
-        picked[g] = jnp.concatenate(accs[g * parts:(g + 1) * parts], axis=0).astype(BF16)
-    for d in range(1, n):
-        row_copy(t, (t + d) % n).start()
-    rows[:, pl.ds(pl.multiple_of(t * LANES, LANES), LANES)] = picked[t // per]
-    for d in range(1, n):
-        row_copy((t + d) % n, t).wait_recv()
+        row_copy(0, (t + d) % n, t).wait_recv()
 
     placed = jnp.dot(rows[...], place[...], preferred_element_type=F32)
     listed[o] = placed.astype(BF16)
@@ -241,7 +274,7 @@
 
     for d in range(1, n):
         req_copy(t, (t + d) % n).wait_send()
-        row_copy(t, (t + d) % n).wait_send()
+        row_copy(0, t, (t + d) % n).wait_send()
     for d in range(1, m):
         occ_copy(o, (o + d) % m).wait_send()
         list_copy(o, (o + d) % m).wait_send()
@@ -267,12 +300,15 @@
     return pl.pallas_call(
         functools.partial(kernel, n, m),
         out_shape=(
-            jax.ShapeDtypeStruct((depth, width, CZ), F32),
-            jax.ShapeDtypeStruct((3, depth, width, CZ), F32),
+            pltpu.VMEM((depth, width, CZ), F32),
+            pltpu.VMEM((3, depth, width, CZ), F32),
         ),
-        in_specs=[vmem, vmem, vmem, hbm, hbm],
+        in_specs=[hbm] * 5,
         out_specs=(vmem, vmem),
         scratch_shapes=[
+            pltpu.VMEM((1, nbt), jnp.int32),
+            pltpu.VMEM((1, nbt), jnp.int32),
+            pltpu.VMEM((1, loc), F32),
             pltpu.VMEM((depth, nbt, (width + 2) * CZ), BF16),
             pltpu.VMEM((loc, held), BF16),
             pltpu.VMEM((n, 8, LANES), jnp.int32),
@@ -283,10 +319,10 @@
             pltpu.VMEM((m, 8, LANES), F32),
             pltpu.VMEM((m, loc, nbt), BF16),
             pltpu.VMEM((depth + 2, width + 16, CZ), F32),
-            dma((depth, 3)), dma(()),
+            dma((3,)), dma((depth, 3)), dma(()),
             dma((n,)), dma((n,)), dma((n,)), dma((n,)),
             dma((m,)), dma((m,)), dma((m,)), dma((m,)),
-            dma((2,)), dma((2,)),
+            dma((2,)), dma((2,)), pltpu.SemaphoreType.REGULAR((max(1, m - 2),)),
         ],
         compiler_params=pltpu.CompilerParams(collective_id=0, has_side_effects=True),
     )(

time: 27.2 us -> 23.9 us (0.88)
  local copies, waits for them, and re-layouts: 3.09 us -> 1.31 us
  Pallas kernels: 23.2 us -> 21.8 us
    unnamed x2, local copies, waits for them, and re-layouts: 3.09 us -> 1.31 us
    pallas_call x1, Pallas kernels: 23.2 us -> 21.8 us  [body(): pl.pallas_call(functools.partial(kernel, n, m), out_shape=(pltpu.VMEM((de...]
where the time goes in v2:
time: 23.9 us; the launch traced here: 23.7 us
  Pallas kernels  21.8 us (91%)
  local copies, waits for them, and re-layouts  1.31 us (5%)
  between operations  0.64 us (3%)
    pallas_call x1, Pallas kernels, body(): pl.pallas_call(functools.partial(kernel, n, m), out_shape=(pltpu.VMEM((de...  21.8 us
    unnamed x2, local copies, waits for them, and re-layouts  1.31 us

profile of v2, /device:TPU:0, one launch (start us, length us, event | category | flops | bytes accessed | tf_op | source)
XLA Modules:
  0.0 23.7 jit_solution(791619648004926854)
XLA Ops:
  0.6 21.8 %shard_map.68 = (f32[8,16,128]{2,1,0:T(8,128)S(1)}, f32[3,8,16,128]{3,2,1,0:T(8,128)S(1)}) custom-call(s32[1,256]{1,0:T(1,128)} %bitcast.5, s32[1,256]{1,0:T(1,128)} %bitcast.6, f32[1,32]{1,0:T(1,128)} %bitcast.7, bf16[32,8192]{1,0:T(8,128)(2,1)} %bitcast.4, bf16[256,65536]{1,0:T(8,128)(2,1)} %basis_ref.1), custom_call_target="tpu_custom_call" | custom-call | tf_op jit(solution)/shard_map/pallas_call | solution.py:300
  22.4 0.6 %copy.9 = f32[8,16,128]{2,1,0:T(8,128)} copy(f32[8,16,128]{2,1,0:T(8,128)S(1)} %get-tuple-element.2) | data formatting | bytes 131072
  23.1 0.7 %copy.10 = f32[3,8,16,128]{3,2,1,0:T(8,128)} copy(f32[3,8,16,128]{3,2,1,0:T(8,128)S(1)} %get-tuple-element.3) | data formatting | bytes 393216
